TPU v7x, 32 devices: a whole 2x2x4 slice. The times are simulated.
32 devices in a mesh: grp: 2 (over y), gx: 4 (over z), gy: 2 (over x), gz: 2 (over core).
Axes of the slice: x: 2, y: 2, z: 4, core: 2. Of those that a mesh axis runs over, the one named last changes fastest.
Arguments:
- snapshot: bfloat16 [2048, 4, 16, 1024], P(('grp', 'gx'), None, 'gz', 'gy'), parts along dimension 0, may hold values from -16 to 16
- x_basis: bfloat16 [2048, 128], P('grp'), parts along dimension 0, may hold values from -0.1875 to 0.1875
- y_basis: bfloat16 [2048, 128], P('grp'), parts along dimension 0, may hold values from -0.1875 to 0.1875
Outputs:
- gram_out: float32 [2048, 1024], P(('grp', 'gx'), ('gy', 'gz')), parts along dimension 0
- core_out: float32 [256, 4, 16, 128], P(('grp', 'gx', 'gy'), None, 'gz'), parts along dimension 0
There are 2 independent parts, one for each index of `grp`. A program takes and returns all parts, laid end to end along the dimension named above; each array names one. Nothing has to cross between parts.
All inputs are finite; a program needn't handle non-finite values.
Results may differ from a plain program's by a relative error of at most 0.0029.
Values may be sent and summed in bfloat16 or wider, within the bound.
No kernel may reach another device: no remote copies, remote signals or barrier semaphores. Data moves between devices by JAX's collectives and lax.ppermute only.
A program may use at most 128 MiB of HBM per device.

v0:
```python
import jax
import jax.numpy as jnp
from jax import lax
from jax.sharding import PartitionSpec as P


def on_device(snapshot, x_basis, y_basis):
    rows_local = snapshot.shape[0]
    columns = snapshot.shape[1] * snapshot.shape[2] * snapshot.shape[3]
    unfolded = snapshot.reshape(rows_local, columns)
    rank_count = x_basis.shape[1]
    across = lax.axis_size("gx")
    rank_rows = rank_count // across
    groups = lax.axis_size("gy") * lax.axis_size("gz")
    inverse = 1.0 / (columns * groups)
    basis_cols = lax.dynamic_slice_in_dim(x_basis, lax.axis_index("gx") * rank_rows, rank_rows, 1)
    shard_rows = lax.all_gather(unfolded, "gx", axis=0, tiled=True)
    gram_block = lax.dot_general(
        unfolded, shard_rows, (((1,), (1,)), ((), ())), preferred_element_type=jnp.float32
    )
    gram_rows = gram_block
    partial_value = lax.dot_general(
        basis_cols, shard_rows, (((0,), (0,)), ((), ())), preferred_element_type=jnp.float32
    )
    gram_rows, partial_value = (gram_rows, partial_value)
    gram_out = lax.psum_scatter(gram_rows * inverse, ("gy", "gz"), scatter_dimension=1, tiled=True)
    own_rows = partial_value.astype(jnp.bfloat16)
    shaped = own_rows.reshape(rank_rows, snapshot.shape[1], snapshot.shape[2], snapshot.shape[3])
    along_y = lax.all_to_all(shaped, "gy", split_axis=0, concat_axis=3, tiled=True)
    core_flat = jnp.dot(
        along_y.reshape(-1, along_y.shape[3]), y_basis, preferred_element_type=jnp.float32
    )
    core_block = core_flat.reshape(
        along_y.shape[0], along_y.shape[1], along_y.shape[2], y_basis.shape[1]
    )
    return (gram_out, core_block)


def solution(mesh):
    in_specs = (P(("grp", "gx"), None, "gz", "gy"), P("grp", None), P("grp", None))
    out_specs = (P(("grp", "gx"), ("gy", "gz")), P(("grp", "gx", "gy"), None, "gz", None))
    return jax.shard_map(
        on_device, mesh=mesh, in_specs=in_specs, out_specs=out_specs, check_vma=False
    )
```

profile of v0, /device:TPU:0, one launch (start us, length us, event | category | flops | bytes accessed | tf_op | source)
XLA Modules:
  0.0 646.1 jit_solution(14155558887606311559)
XLA Ops:
  7.2 0.0 copy-start
  7.2 0.0 all-gather.2.cloned.1.call-start
  7.2 15.4 %copy.7 = bf16[32,8,32,512]{3,1,2,0:T(8,128)(2,1)} copy(bf16[32,8,32,512]{3,2,1,0:T(8,128)(2,1)} %bitcast.21) | data formatting | bytes 16777216
  22.6 0.0 all-gather.2.cloned.1.call-update
  22.6 0.2 reduce-scatter.2.cloned.1.call-start
  22.9 564.0 %all-gather.2.cloned.1.call-done = bf16[1024,16384]{1,0:T(8,128)(2,1)} async-done(((bf16[256,16384]{1,0:T(8,128)(2,1)}), bf16[1024,16384]{1,0:T(8,128)(2,1)}) %all-gather.2.cloned.1.call-update) | async-done | bytes 33554448 | tf_op jit(solution)/shard_map/all_gather | solution.py:17
  586.9 17.6 %convolution_multiply_fusion = f32[256,1024]{1,0:T(8,128)} fusion(bf16[256,16384]{1,0:T(8,128)(2,1)} %bitcast.20, bf16[1024,16384]{1,0:T(8,128)(2,1)} %all-gather.2.cloned.1.call-done), kind=kOutput, calls=%fused_computation.1 | convolution fusion | flops 8590196736 | bytes 42991616 | tf_op jit(solution)/shard_map/dot_general | solution.py:18
  604.5 0.0 copy-start.1
  604.5 0.0 reduce-scatter.2.cloned.1.call-update
  604.5 0.0 copy-done
  604.5 14.4 %convolution_convert_fusion = bf16[32,16384]{1,0:T(8,128)(2,1)S(1)} fusion(bf16[1024,16384]{1,0:T(8,128)(2,1)} %all-gather.2.cloned.1.call-done, bf16[1024,128]{1,0:T(8,128)(2,1)S(1)} %copy-done, s32[]{:T(128)S(6)} %select_n.3), kind=kOutput, calls=%fused_computation | convolution fusion | flops 1074266112 | bytes 34865156 | tf_op jit(solution)/shard_map/dot_general | solution.py:22
  618.9 0.3 copy.8
  619.2 18.8 %all_to_all.15 = bf16[32,4,8,512]{3,2,1,0:T(8,128)(2,1)S(1)} all-to-all(bf16[32,4,8,512]{3,2,1,0:T(8,128)(2,1)S(1)} %bitcast.23), channel_id=1, replica_groups=mesh['grp'=2,'gx'=4,'gy'=2,'gz'=2] {'gy'}, dimensions={0} | all-to-all | bytes 2097152 | tf_op jit(solution)/shard_map/all_to_all | solution.py:29
  638.0 0.1 copy.5
  638.1 0.0 copy-done.1
  638.1 1.1 fusion
  639.2 0.0 reduce-scatter.2.cloned.1.call-done
Async XLA Ops:
  7.2 597.3 %copy-start = (bf16[1024,128]{1,0:T(8,128)(2,1)S(1)}, bf16[1024,128]{1,0:T(8,128)(2,1)}, u32[]{:S(2)}) copy-start(bf16[1024,128]{1,0:T(8,128)(2,1)} %param.4) | copy-start | bytes 786436
  7.2 579.7 %all-gather.2.cloned.1.call-start = ((), (), s32[]{:S(2)}) async-start(), calls=%async_computation.2 | async-start | bytes 41943040 | tf_op jit(solution)/shard_map/all_gather | solution.py:17
  22.6 616.6 %reduce-scatter.2.cloned.1.call-start = ((), (), s32[]{:S(2)}) async-start(), calls=%async_computation.3 | async-start | bytes 1310720 | tf_op jit(solution)/shard_map/reduce_scatter | solution.py:26
  604.5 33.6 %copy-start.1 = (bf16[1024,128]{1,0:T(8,128)(2,1)S(1)}, bf16[1024,128]{1,0:T(8,128)(2,1)}, u32[]{:S(2)}) copy-start(bf16[1024,128]{1,0:T(8,128)(2,1)} %param.5) | copy-start | bytes 786436
Sparse Core Ops, SparseCore 0:
  22.7 564.0 all-gather.1
  604.6 25.1 reduce-scatter.1
where the time goes:
time: 646 us
  waiting for transfers between devices  564 us (87%)
  matrix products  33.1 us (5%)
  blocking collectives  18.8 us (3%)
  local copies, waits for them, and re-layouts  15.8 us (2%)
  between operations  14.1 us (2%)
    all_gather x1, waiting for transfers between devices, on_device(): shard_rows = lax.all_gather(unfolded, 'gx', axis=0, tiled=True)  564 us
    all_to_all x1, blocking collectives, on_device(): lax.all_to_all(shaped, 'gy', split_axis=0, concat_axis=3, tiled=True)  18.8 us
    dot_general x1, matrix products, on_device(): lax.dot_general(unfolded, shard_rows, (((1,), (1,)), ((), ())), preferred...  17.6 us
    unnamed x6, local copies, waits for them, and re-layouts  15.7 us
    dot_general x1, matrix products, on_device(): lax.dot_general(basis_cols, shard_rows, (((0,), (0,)), ((), ())), preferr...  14.4 us
  transfers between devices with their start and end apart: 2, of which 1 were waited for; matrix products, arithmetic and copies ran while one was open for 2% of the time, Pallas kernels for 0%

commit v1 on v0

--- a/solution.py
+++ b/solution.py
@@ -14,7 +14,12 @@
     groups = lax.axis_size("gy") * lax.axis_size("gz")
     inverse = 1.0 / (columns * groups)
     basis_cols = lax.dynamic_slice_in_dim(x_basis, lax.axis_index("gx") * rank_rows, rank_rows, 1)
-    shard_rows = lax.all_gather(unfolded, "gx", axis=0, tiled=True)
+    ring = [unfolded]
+    for hop in range(3):
+        ring.append(lax.ppermute(ring[-1], "gx", [(dev, (dev + 1) % 4) for dev in range(4)]))
+    shard_rows = jnp.roll(
+        jnp.concatenate(ring[::-1], axis=0), (lax.axis_index("gx") + 1) * ring[0].shape[0], axis=0
+    )
     gram_block = lax.dot_general(
         unfolded, shard_rows, (((1,), (1,)), ((), ())), preferred_element_type=jnp.float32
     )

time: 646 us -> 700 us (1.084)
  local copies, waits for them, and re-layouts: 15.8 us -> 80.8 us
  waiting for transfers between devices: 564 us -> 549 us
    all_gather x1 -> x0, waiting for transfers between devices: 564 us -> none  [on_device(): shard_rows = lax.all_gather(unfolded, 'gx', axis=0, tiled=True)]
    ppermute x0 -> x3, waiting for transfers between devices: none -> 549 us  [on_device(): lax.ppermute(ring[-1], 'gx', [(dev, (dev + 1) % 4) for dev in range(4)])]
    unnamed x6 -> x16, local copies, waits for them, and re-layouts: 15.7 us -> 73.2 us
    concatenate x0 -> x1, local copies, waits for them, and re-layouts: none -> 7.47 us  [on_device(): jnp.roll(jnp.concatenate(ring[::-1], axis=0), (lax.axis_index('gx') + 1)...]
  transfers between devices with their start and end apart: 2 -> 4, of which waited for: 1 -> 3; matrix products, arithmetic and copies ran while one was open for 2% -> 2% of each run, Pallas kernels for 0% -> 0%
where the time goes in v1:
time: 700 us; the launch traced here: 699 us
  waiting for transfers between devices  549 us (78%)
  local copies, waits for them, and re-layouts  80.8 us (12%)
  matrix products  33.7 us (5%)
  blocking collectives  18.3 us (3%)
  between operations  14.1 us (2%)
    ppermute x3, waiting for transfers between devices, on_device(): lax.ppermute(ring[-1], 'gx', [(dev, (dev + 1) % 4) for dev in range(4)])  549 us
    unnamed x16, local copies, waits for them, and re-layouts  73.2 us
    all_to_all x1, blocking collectives, on_device(): lax.all_to_all(shaped, 'gy', split_axis=0, concat_axis=3, tiled=True)  18.3 us
    dot_general x1, matrix products, on_device(): lax.dot_general(unfolded, shard_rows, (((1,), (1,)), ((), ())), preferred...  18.3 us
    dot_general x1, matrix products, on_device(): lax.dot_general(basis_cols, shard_rows, (((0,), (0,)), ((), ())), preferr...  14.3 us
  transfers between devices with their start and end apart: 4, of which 3 were waited for; matrix products, arithmetic and copies ran while one was open for 2% of the time, Pallas kernels for 0%

profile of v1, /device:TPU:0, one launch (start us, length us, event | category | flops | bytes accessed | tf_op | source)
XLA Modules:
  0.0 699.0 jit_solution(246916528687135657)
XLA Ops:
  7.2 0.0 copy-start
  7.2 0.0 reduce-scatter.2.cloned.1.call-start
  7.2 15.4 %copy.8 = bf16[32,8,32,512]{3,1,2,0:T(8,128)(2,1)} copy(bf16[32,8,32,512]{3,2,1,0:T(8,128)(2,1)} %bitcast.23) | data formatting | bytes 16777216
  22.6 3.0 collective-permute-start
  25.6 182.7 %collective-permute-done = bf16[256,16384]{1,0:T(8,128)(2,1)S(1)} collective-permute-done((bf16[256,16384]{1,0:T(8,128)(2,1)}, bf16[256,16384]{1,0:T(8,128)(2,1)S(1)}, u32[]{:S(2)}, u32[]{:S(2)}) %collective-permute-start) | collective-permute-done | bytes 8388640 | tf_op jit(solution)/shard_map/ppermute | solution.py:19
  208.3 3.3 copy-done.1
  211.6 183.5 %collective-permute-done.1 = bf16[256,16384]{1,0:T(8,128)(2,1)} collective-permute-done((bf16[256,16384]{1,0:T(8,128)(2,1)S(1)}, bf16[256,16384]{1,0:T(8,128)(2,1)}, u32[]{:S(2)}, u32[]{:S(2)}) %collective-permute-start.1) | collective-permute-done | bytes 8388640 | tf_op jit(solution)/shard_map/ppermute | solution.py:19
  395.2 182.8 %collective-permute-done.2 = bf16[256,16384]{1,0:T(8,128)(2,1)} collective-permute-done((bf16[256,16384]{1,0:T(8,128)(2,1)}, bf16[256,16384]{1,0:T(8,128)(2,1)}, u32[]{:S(2)}, u32[]{:S(2)}) %collective-permute-start.2) | collective-permute-done | bytes 8388640 | tf_op jit(solution)/shard_map/ppermute | solution.py:19
  578.0 7.5 %constant_dynamic-update-slice_fusion.7 = bf16[2048,16384]{1,0:T(8,128)(2,1)} fusion(bf16[256,16384]{1,0:T(8,128)(2,1)} %collective-permute-done.2), kind=kLoop, calls=%fused_computation.17 | loop fusion | bytes 16777216
  585.5 7.5 %constant_dynamic-update-slice_fusion.6 = bf16[2048,16384]{1,0:T(8,128)(2,1)} fusion(bf16[2048,16384]{1,0:T(8,128)(2,1)} %constant_dynamic-update-slice_fusion.7, bf16[256,16384]{1,0:T(8,128)(2,1)} %collective-permute-done.1), kind=kLoop, calls=%fused_computation.16 | loop fusion | bytes 16777216
  593.0 7.5 %constant_dynamic-update-slice_fusion.5 = bf16[2048,16384]{1,0:T(8,128)(2,1)} fusion(bf16[2048,16384]{1,0:T(8,128)(2,1)} %constant_dynamic-update-slice_fusion.6, bf16[256,16384]{1,0:T(8,128)(2,1)} %copy-done.1), kind=kLoop, calls=%fused_computation.15 | loop fusion | bytes 16777216
  600.4 7.5 %constant_dynamic-update-slice_fusion.4 = bf16[2048,16384]{1,0:T(8,128)(2,1)} fusion(bf16[2048,16384]{1,0:T(8,128)(2,1)} %constant_dynamic-update-slice_fusion.5, bf16[256,16384]{1,0:T(8,128)(2,1)} %bitcast.20), kind=kLoop, calls=%fused_computation.14 | loop fusion | bytes 16777216
  607.9 7.5 %constant_dynamic-update-slice_fusion.3 = bf16[2048,16384]{1,0:T(8,128)(2,1)} fusion(bf16[2048,16384]{1,0:T(8,128)(2,1)} %constant_dynamic-update-slice_fusion.4, bf16[256,16384]{1,0:T(8,128)(2,1)} %collective-permute-done.2), kind=kLoop, calls=%fused_computation.13 | loop fusion | bytes 16777216
  615.4 7.5 %constant_dynamic-update-slice_fusion.2 = bf16[2048,16384]{1,0:T(8,128)(2,1)} fusion(bf16[2048,16384]{1,0:T(8,128)(2,1)} %constant_dynamic-update-slice_fusion.3, bf16[256,16384]{1,0:T(8,128)(2,1)} %collective-permute-done.1), kind=kLoop, calls=%fused_computation.12 | loop fusion | bytes 16777216
  622.9 7.5 %constant_dynamic-update-slice_fusion.1 = bf16[2048,16384]{1,0:T(8,128)(2,1)} fusion(bf16[2048,16384]{1,0:T(8,128)(2,1)} %constant_dynamic-update-slice_fusion.2, bf16[256,16384]{1,0:T(8,128)(2,1)} %copy-done.1), kind=kLoop, calls=%fused_computation.11 | loop fusion | bytes 16777216
  630.4 7.5 %constant_dynamic-update-slice_fusion = bf16[2048,16384]{1,0:T(8,128)(2,1)} fusion(bf16[2048,16384]{1,0:T(8,128)(2,1)} %constant_dynamic-update-slice_fusion.1, bf16[256,16384]{1,0:T(8,128)(2,1)} %bitcast.21), kind=kLoop, calls=%fused_computation.10 | loop fusion | bytes 16777216 | tf_op jit(solution)/shard_map/jit(_roll_dynamic)/concatenate | solution.py:20
  637.9 18.3 %fusion.10 = f32[256,1024]{0,1:T(8,128)} fusion(bf16[256,16384]{1,0:T(8,128)(2,1)} %bitcast.22, bf16[2048,16384]{1,0:T(8,128)(2,1)} %constant_dynamic-update-slice_fusion, s32[]{:T(128)S(6)} %select_n.17), kind=kOutput, calls=%fused_computation.6 | convolution fusion | flops 8590196736 | bytes 42991620 | tf_op jit(solution)/shard_map/dot_general | solution.py:23
  656.1 0.0 reduce-scatter.2.cloned.1.call-update
  656.1 14.3 %fusion.4 = bf16[32,16384]{1,0:T(8,128)(2,1)S(1)} fusion(bf16[2048,16384]{1,0:T(8,128)(2,1)} %constant_dynamic-update-slice_fusion, s32[]{:T(128)S(6)} %select_n.17, bf16[1024,128]{1,0:T(8,128)(2,1)S(1)} %copy-done, s32[]{:T(128)S(6)} %select_n.18), kind=kOutput, calls=%fused_computation.4 | convolution fusion | flops 1074266112 | bytes 34865160 | tf_op jit(solution)/shard_map/dot_general | solution.py:27
  670.5 0.3 copy.9
  670.8 18.3 %all_to_all.15 = bf16[32,4,8,512]{3,2,1,0:T(8,128)(2,1)S(1)} all-to-all(bf16[32,4,8,512]{3,2,1,0:T(8,128)(2,1)S(1)} %bitcast.25), channel_id=1, replica_groups=mesh['grp'=2,'gx'=4,'gy'=2,'gz'=2] {'gy'}, dimensions={0} | all-to-all | bytes 2097152 | tf_op jit(solution)/shard_map/all_to_all | solution.py:34
  689.1 0.1 copy.5
  689.3 1.1 fusion.13
  690.4 1.8 copy.6
  (7 shorter events, 0.0 us)
Async XLA Ops:
  7.2 649.0 %copy-start = (bf16[1024,128]{1,0:T(8,128)(2,1)S(1)}, bf16[1024,128]{1,0:T(8,128)(2,1)}, u32[]{:S(2)}) copy-start(bf16[1024,128]{1,0:T(8,128)(2,1)} %param.4) | copy-start | bytes 786436
  7.2 683.2 %reduce-scatter.2.cloned.1.call-start = ((), (), s32[]{:S(2)}) async-start(), calls=%async_computation.2 | async-start | bytes 1310720 | tf_op jit(solution)/shard_map/reduce_scatter | solution.py:31
  22.6 185.7 %collective-permute-start = (bf16[256,16384]{1,0:T(8,128)(2,1)}, bf16[256,16384]{1,0:T(8,128)(2,1)S(1)}, u32[]{:S(2)}, u32[]{:S(2)}) collective-permute-start(bf16[256,16384]{1,0:T(8,128)(2,1)} %bitcast.19), channel_id=1, source_target_pairs={{0,4},{4,8},{8,12},{12,0},{1,5},{5,9},{9,13},{13,1},{2,6},{6,10},{... | collective-permute-start | bytes 25165832 | tf_op jit(solution)/shard_map/ppermute | solution.py:19
  208.3 3.3 copy-start.1
  211.6 183.5 %collective-permute-start.1 = (bf16[256,16384]{1,0:T(8,128)(2,1)S(1)}, bf16[256,16384]{1,0:T(8,128)(2,1)}, u32[]{:S(2)}, u32[]{:S(2)}) collective-permute-start(bf16[256,16384]{1,0:T(8,128)(2,1)S(1)} %collective-permute-done), channel_id=1, source_target_pairs={{0,4},{4,8},{8,12},{12,0},{1,5},{5,9},{9,13},{13,1},{2,6},{6,10},{... | collective-permute-start | bytes 25165832 | tf_op jit(solution)/shard_map/ppermute | solution.py:19
  395.2 182.8 %collective-permute-start.2 = (bf16[256,16384]{1,0:T(8,128)(2,1)}, bf16[256,16384]{1,0:T(8,128)(2,1)}, u32[]{:S(2)}, u32[]{:S(2)}) collective-permute-start(bf16[256,16384]{1,0:T(8,128)(2,1)} %collective-permute-done.1), channel_id=1, source_target_pairs={{0,4},{4,8},{8,12},{12,0},{1,5},{5,9},{9,13},{13,1},{2,6},{6,10},{... | collective-permute-start | bytes 25165832 | tf_op jit(solution)/shard_map/ppermute | solution.py:19
  622.9 66.4 %copy-start.2 = (bf16[1024,128]{1,0:T(8,128)(2,1)S(1)}, bf16[1024,128]{1,0:T(8,128)(2,1)}, u32[]{:S(2)}) copy-start(bf16[1024,128]{1,0:T(8,128)(2,1)} %param.5) | copy-start | bytes 786436
Sparse Core Ops, SparseCore 0:
  656.3 26.1 reduce-scatter.1
